TPU v7x, 32 devices: a whole 2x2x4 slice. The times are simulated.
32 devices in a mesh: dp: 2 (over y), table: 16 (over z, x, core).
Axes of the slice: x: 2, y: 2, z: 4, core: 2. Of those that a mesh axis runs over, the one named last changes fastest.
Arguments:
- gradients: bfloat16 [256, 4096], P(None, ('dp', 'table')), may hold values from -16 to 16
- row_ids: int32 [4096], P(('dp', 'table')), may hold values from 0 to 32767
- table_block: float32 [256, 32768], P('table', 'dp'), may hold values from -6 to 6
- adagrad_state: float32 [32768], P('dp'), may hold values from 0.05 to 2
Outputs:
- new_table: float32 [256, 32768], P('table', 'dp')
- new_state: float32 [32768], P('dp')
All inputs are finite; a program needn't handle non-finite values.
Results may differ from a plain program's by a relative error of at most 0.0003.
Values may be sent and summed in bfloat16 or wider, within the bound.
A program may use at most 64 MiB of HBM per device.

v0:
```python
import jax
import jax.numpy as jnp
from jax import lax
from jax.sharding import PartitionSpec as P

W = 256
learn_rate = 0.5


def accumulate(grads, ids, first_row, count_rows):
    relative = ids - first_row
    inside = (relative >= 0) & (relative < count_rows)
    target = jnp.where(inside, relative, count_rows)
    start_total = jnp.zeros((grads.shape[0], count_rows), jnp.float32)
    return start_total.at[:, target].add(grads.astype(jnp.float32), mode="drop")


def body(gradients, row_ids, table_block, adagrad_state):
    owned = lax.all_to_all(gradients, "table", split_axis=0, concat_axis=1, tiled=True)
    local_rows = table_block.shape[1]
    all_row_ids = lax.all_gather(row_ids, ("dp", "table"), axis=0, tiled=True)
    first_row = lax.axis_index("dp") * local_rows
    row_grad = accumulate(
        lax.all_gather(owned, "dp", axis=1, tiled=True), all_row_ids, first_row, local_rows
    )
    partial_squares = jnp.sum(row_grad * row_grad, axis=0)
    squares = lax.psum(partial_squares, "table")
    new_state = adagrad_state + squares / W
    new_table = table_block - learn_rate * row_grad / jnp.sqrt(new_state)[None, :]
    return (new_table, new_state)


def solution(mesh):
    in_specs = (P(None, ("dp", "table")), P(("dp", "table")), P("table", "dp"), P("dp"))
    out_specs = (P("table", "dp"), P("dp"))
    return jax.shard_map(body, mesh=mesh, in_specs=in_specs, out_specs=out_specs, check_vma=False)
```

profile of v0, /device:TPU:8, one launch (start us, length us, event | category | flops | bytes accessed | tf_op | source)
XLA Modules:
  0.0 214.5 jit_solution(18062439507933522561)
XLA Ops:
  7.2 6.3 %all-to-all-start = ((bf16[16,16,128]{2,1,0:T(8,128)(2,1)}), bf16[16,16,128]{2,1,0:T(8,128)(2,1)S(1)}, u32[]{:S(2)}, u32[]{:S(2)}) async-start(bf16[16,16,128]{2,1,0:T(8,128)(2,1)} %bitcast.12), calls=%async_computation | async-start | bytes 131072 | tf_op jit(solution)/shard_map/all_to_all | solution.py:19
  13.4 0.0 all-reduce.2.cloned.1.call-start
  13.5 38.0 %all-gather = s32[32,1,128]{2,1,0:T(1,128)S(1)} all-gather(s32[1,1,128]{2,1,0:T(1,128)} %bitcast.15), channel_id=1, replica_groups=mesh['dp'=2,'table'=16] {'dp','table'}, dimensions={0}, use_global_device_ids=true | all-gather | bytes 16896 | tf_op jit(solution)/shard_map/all_gather | solution.py:21
  51.5 0.0 all-to-all-done
  51.5 0.3 copy.9
  51.8 14.8 %all_gather.7 = bf16[16,4096]{0,1:T(8,128)(2,1)S(1)} all-gather(bf16[16,2048]{0,1:T(8,128)(2,1)S(1)} %bitcast.10), channel_id=1, replica_groups=mesh['dp'=2,'table'=16] {'dp'}, dimensions={1}, use_global_device_ids=true | all-gather | bytes 196608 | tf_op jit(solution)/shard_map/all_gather | solution.py:24
  66.7 0.0 copy-start
  66.7 26.1 %scatter_custom_fusion = f32[16,16384]{0,1:T(8,128)} fusion(s32[4096]{0:T(1024)S(1)} %compare_select_fusion, f32[]{:T(128)} %constant.7.clone.1, bf16[16,4096]{0,1:T(8,128)(2,1)S(1)} %all_gather.7), kind=kCustom, calls=%fused_computation.3 | custom fusion | flops 131072 | bytes 2097156 | tf_op jit(solution)/shard_map/scatter-add | solution.py:15
  92.8 0.0 copy-start.1
  92.8 5.3 %multiply_reduce_fusion = f32[16384]{0:T(1024)} fusion(f32[16,16384]{0,1:T(8,128)} %scatter_custom_fusion), kind=kLoop, calls=%fused_computation.2 | loop fusion | flops 507904 | bytes 1114112 | tf_op jit(solution)/shard_map/reduce_sum | solution.py:26
  98.1 0.0 all-reduce.2.cloned.1.call-update
  98.1 0.0 copy-done
  98.1 4.6 %copy.10 = f32[16,16384]{0,1:T(8,128)} copy(f32[16,16384]{1,0:T(8,128)S(1)} %copy-done) | data formatting | bytes 2097152 | tf_op args[2]
  102.7 84.2 %all-reduce.2.cloned.1.call-done = f32[16384]{0:T(1024)} async-done(((f32[16384]{0:T(1024)}), f32[16384]{0:T(1024)}) %all-reduce.2.cloned.1.call-update) | async-done | bytes 65552 | tf_op jit(solution)/shard_map/psum | solution.py:27
  186.9 0.0 copy-done.1
  186.9 1.5 fusion.4
  188.4 13.3 %divide_subtract_fusion = f32[16,16384]{0,1:T(8,128)} fusion(f32[16,16384]{0,1:T(8,128)} %copy.10, f32[16,16384]{0,1:T(8,128)} %scatter_custom_fusion, f32[16384]{0:T(1024)S(1)} %get-tuple-element.6), kind=kLoop, calls=%fused_computation.1 | loop fusion | flops 786432 | bytes 3211264 | tf_op jit(solution)/shard_map/sub | solution.py:29
  201.7 6.0 %copy.11 = f32[16,16384]{1,0:T(8,128)} copy(f32[16,16384]{0,1:T(8,128)} %divide_subtract_fusion) | data formatting | bytes 2097152
  (2 shorter events, 0.0 us)
Async XLA Ops:
  7.2 44.4 %all-to-all-start = ((bf16[16,16,128]{2,1,0:T(8,128)(2,1)}), bf16[16,16,128]{2,1,0:T(8,128)(2,1)S(1)}, u32[]{:S(2)}, u32[]{:S(2)}) async-start(bf16[16,16,128]{2,1,0:T(8,128)(2,1)} %bitcast.12), calls=%async_computation | async-start | bytes 131072 | tf_op jit(solution)/shard_map/all_to_all | solution.py:19
  13.4 173.5 %all-reduce.2.cloned.1.call-start = ((), (), s32[]{:S(2)}) async-start(), calls=%async_computation.1 | async-start | bytes 131072 | tf_op jit(solution)/shard_map/psum | solution.py:27
  66.7 31.4 %copy-start = (f32[16,16384]{1,0:T(8,128)S(1)}, f32[16,16384]{1,0:T(8,128)}, u32[]{:S(2)}) copy-start(f32[16,16384]{1,0:T(8,128)} %param.6) | copy-start | bytes 3145732
  92.8 94.1 %copy-start.1 = (f32[16384]{0:T(1024)S(1)}, f32[16384]{0:T(1024)}, u32[]{:S(2)}) copy-start(f32[16384]{0:T(1024)} %param.7) | copy-start | bytes 196612
Sparse Core Ops, SparseCore 0:
  98.2 88.6 all-reduce.1
where the time goes:
time: 215 us
  waiting for transfers between devices  84.2 us (39%)
  blocking collectives  52.9 us (25%)
  other arithmetic  46.2 us (21%)
  between operations  14.1 us (7%)
  local copies, waits for them, and re-layouts  10.9 us (5%)
  starting transfers between devices  6.32 us (3%)
    psum x1, waiting for transfers between devices, body(): squares = lax.psum(partial_squares, 'table')  84.2 us
    all_gather x1, blocking collectives, body(): all_row_ids = lax.all_gather(row_ids, ('dp', 'table'), axis=0, tiled=True)  38 us
    scatter-add x1, other arithmetic, accumulate(): return start_total.at[:, target].add(grads.astype(jnp.float32), mode='drop')  26.1 us
    all_gather x1, blocking collectives, body(): lax.all_gather(owned, 'dp', axis=1, tiled=True)  14.8 us
    sub x1, other arithmetic, body(): table_block - learn_rate * row_grad / jnp.sqrt(new_state)[None, :]  13.3 us
    unnamed x6, local copies, waits for them, and re-layouts  10.6 us
    all_to_all x1, starting transfers between devices, body(): lax.all_to_all(gradients, 'table', split_axis=0, concat_axis=1, tiled=True)  6.28 us
    reduce_sum x1, other arithmetic, body(): partial_squares = jnp.sum(row_grad * row_grad, axis=0)  5.28 us
  transfers between devices with their start and end apart: 2, of which 1 were waited for; matrix products, arithmetic and copies ran while one was open for 2% of the time, Pallas kernels for 0%

commit v1 on v0

--- a/solution.py
+++ b/solution.py
@@ -5,6 +5,14 @@
 
 W = 256
 learn_rate = 0.5
+
+
+def doubling_sum(shard, name):
+    size, summed = (lax.axis_size(name), shard)
+    for reach in [1 << k for k in range(size.bit_length() - 1)]:
+        pairs = [(i, i ^ reach) for i in range(size)]
+        summed = summed + lax.ppermute(summed, name, pairs)
+    return summed
 
 
 def accumulate(grads, ids, first_row, count_rows):
@@ -24,7 +32,7 @@
         lax.all_gather(owned, "dp", axis=1, tiled=True), all_row_ids, first_row, local_rows
     )
     partial_squares = jnp.sum(row_grad * row_grad, axis=0)
-    squares = lax.psum(partial_squares, "table")
+    squares = doubling_sum(partial_squares, "table")
     new_state = adagrad_state + squares / W
     new_table = table_block - learn_rate * row_grad / jnp.sqrt(new_state)[None, :]
     return (new_table, new_state)

time: 215 us -> 132 us (0.61)
  the two profiles are of different devices: /device:TPU:8 before, /device:TPU:0 now
where the time goes in v1:
time: 132 us; the launch traced here: 131 us
  blocking collectives  56.9 us (43%)
  other arithmetic  44.7 us (34%)
  local copies, waits for them, and re-layouts  10.9 us (8%)
  waiting for transfers between devices  10.4 us (8%)
  starting transfers between devices  7.68 us (6%)
    all_gather x1, blocking collectives, body(): all_row_ids = lax.all_gather(row_ids, ('dp', 'table'), axis=0, tiled=True)  42.1 us
    scatter-add x1, other arithmetic, accumulate(): return start_total.at[:, target].add(grads.astype(jnp.float32), mode='drop')  26.1 us
    all_gather x1, blocking collectives, body(): lax.all_gather(owned, 'dp', axis=1, tiled=True)  14.8 us
    sub x1, other arithmetic, body(): table_block - learn_rate * row_grad / jnp.sqrt(new_state)[None, :]  13.3 us
    unnamed x6, local copies, waits for them, and re-layouts  10.6 us
    ppermute x4, waiting for transfers between devices, doubling_sum(): summed = summed + lax.ppermute(summed, name, pairs)  10.4 us
    all_to_all x1, starting transfers between devices, body(): lax.all_to_all(gradients, 'table', split_axis=0, concat_axis=1, tiled=True)  7.4 us
    reduce_sum x1, other arithmetic, body(): partial_squares = jnp.sum(row_grad * row_grad, axis=0)  4.65 us
  transfers between devices with their start and end apart: 5, of which 4 were waited for; matrix products, arithmetic and copies ran while one was open for 4% of the time, Pallas kernels for 0%

profile of v1, /device:TPU:0, one launch (start us, length us, event | category | flops | bytes accessed | tf_op | source)
XLA Modules:
  0.0 131.3 jit_solution(17381492449079272449)
XLA Ops:
  0.6 7.4 %all-to-all-start = ((bf16[16,16,128]{2,1,0:T(8,128)(2,1)}), bf16[16,16,128]{2,1,0:T(8,128)(2,1)S(1)}, u32[]{:S(2)}, u32[]{:S(2)}) async-start(bf16[16,16,128]{2,1,0:T(8,128)(2,1)} %bitcast.12), calls=%async_computation | async-start | bytes 131072 | tf_op jit(solution)/shard_map/all_to_all | solution.py:27
  8.0 42.1 %all-gather = s32[32,1,128]{2,1,0:T(1,128)S(1)} all-gather(s32[1,1,128]{2,1,0:T(1,128)} %bitcast.15), channel_id=1, replica_groups=mesh['dp'=2,'table'=16] {'dp','table'}, dimensions={0}, use_global_device_ids=true | all-gather | bytes 16896 | tf_op jit(solution)/shard_map/all_gather | solution.py:29
  50.1 0.0 all-to-all-done
  50.1 0.3 copy.9
  50.4 14.8 %all_gather.7 = bf16[16,4096]{0,1:T(8,128)(2,1)S(1)} all-gather(bf16[16,2048]{0,1:T(8,128)(2,1)S(1)} %bitcast.10), channel_id=1, replica_groups=mesh['dp'=2,'table'=16] {'dp'}, dimensions={1}, use_global_device_ids=true | all-gather | bytes 196608 | tf_op jit(solution)/shard_map/all_gather | solution.py:32
  65.2 0.0 copy-start
  65.2 26.1 %scatter_custom_fusion = f32[16,16384]{0,1:T(8,128)} fusion(s32[4096]{0:T(1024)S(1)} %compare_select_fusion, f32[]{:T(128)} %constant.7.clone.1, bf16[16,4096]{0,1:T(8,128)(2,1)S(1)} %all_gather.7), kind=kCustom, calls=%fused_computation.3 | custom fusion | flops 131072 | bytes 2097156 | tf_op jit(solution)/shard_map/scatter-add | solution.py:23
  91.4 0.0 copy-start.1
  91.4 4.6 %multiply_reduce_fusion = f32[16384]{0:T(1024)S(1)} fusion(f32[16,16384]{0,1:T(8,128)} %scatter_custom_fusion), kind=kLoop, calls=%fused_computation.2 | loop fusion | flops 507904 | bytes 1114112 | tf_op jit(solution)/shard_map/reduce_sum | solution.py:34
  96.0 0.1 collective-permute-start
  96.1 1.2 collective-permute-done
  97.3 0.1 collective-permute-start.1
  97.4 4.3 %collective-permute-done.1 = f32[16384]{0:T(1024)S(1)} collective-permute-done((f32[16384]{0:T(1024)S(1)}, f32[16384]{0:T(1024)S(1)}, u32[]{:S(2)}, u32[]{:S(2)}) %collective-permute-start.1) | collective-permute-done | bytes 65568 | tf_op jit(solution)/shard_map/ppermute | solution.py:14
  101.7 0.1 collective-permute-start.2
  101.8 4.3 %collective-permute-done.2 = f32[16384]{0:T(1024)S(1)} collective-permute-done((f32[16384]{0:T(1024)S(1)}, f32[16384]{0:T(1024)S(1)}, u32[]{:S(2)}, u32[]{:S(2)}) %collective-permute-start.2) | collective-permute-done | bytes 65568 | tf_op jit(solution)/shard_map/ppermute | solution.py:14
  106.0 0.1 collective-permute-start.3
  106.1 0.0 copy-done
  106.1 4.6 %copy.10 = f32[16,16384]{0,1:T(8,128)} copy(f32[16,16384]{1,0:T(8,128)S(1)} %copy-done) | data formatting | bytes 2097152 | tf_op args[2]
  110.7 0.7 collective-permute-done.3
  111.4 0.0 copy-done.1
  111.4 0.7 fusion.4
  112.1 13.3 %divide_subtract_fusion = f32[16,16384]{0,1:T(8,128)} fusion(f32[16,16384]{0,1:T(8,128)} %copy.10, f32[16,16384]{0,1:T(8,128)} %scatter_custom_fusion, f32[16384]{0:T(1024)S(1)} %get-tuple-element.6), kind=kLoop, calls=%fused_computation.1 | loop fusion | flops 786432 | bytes 3211264 | tf_op jit(solution)/shard_map/sub | solution.py:37
  125.3 6.0 %copy.11 = f32[16,16384]{1,0:T(8,128)} copy(f32[16,16384]{0,1:T(8,128)} %divide_subtract_fusion) | data formatting | bytes 2097152
  (5 shorter events, 0.0 us)
Async XLA Ops:
  0.6 49.5 %all-to-all-start = ((bf16[16,16,128]{2,1,0:T(8,128)(2,1)}), bf16[16,16,128]{2,1,0:T(8,128)(2,1)S(1)}, u32[]{:S(2)}, u32[]{:S(2)}) async-start(bf16[16,16,128]{2,1,0:T(8,128)(2,1)} %bitcast.12), calls=%async_computation | async-start | bytes 131072 | tf_op jit(solution)/shard_map/all_to_all | solution.py:27
  65.2 40.9 %copy-start = (f32[16,16384]{1,0:T(8,128)S(1)}, f32[16,16384]{1,0:T(8,128)}, u32[]{:S(2)}) copy-start(f32[16,16384]{1,0:T(8,128)} %param.6) | copy-start | bytes 3145732
  91.4 20.1 %copy-start.1 = (f32[16384]{0:T(1024)S(1)}, f32[16384]{0:T(1024)}, u32[]{:S(2)}) copy-start(f32[16384]{0:T(1024)} %param.7) | copy-start | bytes 196612
  96.0 1.3 %collective-permute-start = (f32[16384]{0:T(1024)S(1)}, f32[16384]{0:T(1024)S(1)}, u32[]{:S(2)}, u32[]{:S(2)}) collective-permute-start(f32[16384]{0:T(1024)S(1)} %multiply_reduce_fusion), channel_id=1, source_target_pairs={{0,1},{1,0},{2,3},{3,2},{4,5},{5,4},{6,7},{7,6},{8,9},{9,8},{10,11... | collective-permute-start | bytes 196616 | tf_op jit(solution)/shard_map/ppermute | solution.py:14
  97.3 4.3 %collective-permute-start.1 = (f32[16384]{0:T(1024)S(1)}, f32[16384]{0:T(1024)S(1)}, u32[]{:S(2)}, u32[]{:S(2)}) collective-permute-start(f32[16384]{0:T(1024)S(1)} %add.21), channel_id=1, source_target_pairs={{0,2},{1,3},{2,0},{3,1},{4,6},{5,7},{6,4},{7,5},{8,10},{9,11},{10,... | collective-permute-start | bytes 196616 | tf_op jit(solution)/shard_map/ppermute | solution.py:14
  101.7 4.3 %collective-permute-start.2 = (f32[16384]{0:T(1024)S(1)}, f32[16384]{0:T(1024)S(1)}, u32[]{:S(2)}, u32[]{:S(2)}) collective-permute-start(f32[16384]{0:T(1024)S(1)} %add.22), channel_id=1, source_target_pairs={{0,4},{1,5},{2,6},{3,7},{4,0},{5,1},{6,2},{7,3},{8,12},{9,13},{10,... | collective-permute-start | bytes 196616 | tf_op jit(solution)/shard_map/ppermute | solution.py:14
  106.0 5.4 %collective-permute-start.3 = (f32[16384]{0:T(1024)S(1)}, f32[16384]{0:T(1024)S(1)}, u32[]{:S(2)}, u32[]{:S(2)}) collective-permute-start(f32[16384]{0:T(1024)S(1)} %add.23), channel_id=1, source_target_pairs={{0,8},{1,9},{2,10},{3,11},{4,12},{5,13},{6,14},{7,15},{8,0},{9,1},... | collective-permute-start | bytes 196616 | tf_op jit(solution)/shard_map/ppermute | solution.py:14
